TPU v7x, 32 devices: a whole 2x2x4 slice. The times are simulated.
32 devices in a mesh: row: 4 (over y, x), col: 8 (over z, core).
Axes of the slice: x: 2, y: 2, z: 4, core: 2. Of those that a mesh axis runs over, the one named last changes fastest.
Arguments:
- pointmaps: bfloat16 [64, 64, 2, 3, 14336], P('row', 'col'), may hold values from -6 to 6
- confidence: bfloat16 [64, 64, 2, 14336], P('row', 'col'), may hold values from 1 to 10
- valid_blocks: int32 [64, 64, 64], P('row', 'col'), may hold values 0 or 1
- log_depth: float32 [64, 14336], P('row', 'col'), may hold values from 0 to 1.4
- camera: float32 [64, 8], replicated, may hold values from -1 to 5.8, as said below
- pair_pose: float32 [64, 64, 8], P('row', 'col'), may hold values from -1 to 1.2, as said below
- step_sizes: float32 [3], replicated, may hold values from 0.02 to 0.2
Outputs:
- new_log_depth: float32 [64, 14336], P('row', 'col')
- new_camera: float32 [64, 8], replicated
- new_pair_pose: float32 [64, 64, 8], P('row', 'col')
Inputs may be any that keep to these rules, and one draw needn't show every extreme that they name: `camera`: columns 0 to 3 hold a quaternion whose first entry lies in 0.8 to 1.2 and the others in -0.3 to 0.3; columns 4 to 6 a translation in -1 to 1; column 7 a log focal length in pixels, 5.2 to 5.8. `pair_pose`: columns 0 to 3 hold a quaternion whose first entry lies in 0.8 to 1.2 and the others in -0.3 to 0.3; columns 4 to 6 a translation in -1 to 1; column 7 a log scale in -0.5 to 0.5.
All inputs are finite; a program needn't handle non-finite values. No bound on the sum of `valid_blocks` on one device may be relied on, other than what follows from the above.
Results may differ from a plain program's by a relative error of at most 0.00055.
Values sent between devices are 32-bit elements; how exact they have to be, the bound alone decides.
No kernel may reach another device: no remote copies, remote signals or barrier semaphores. Data moves between devices by JAX's collectives and lax.ppermute only.
A program may use at most 192 MiB of HBM per device.

v0:
```python
import jax
import jax.numpy as jnp
from jax import lax
from jax.sharding import PartitionSpec as P

IMAGES = 64
IMG_WIDTH = 224
IMG_HEIGHT = 224
WIN_ROWS = 64
ADAM_STEPS = 2
BETA_ONE = 0.9
BETA_TWO = 0.999
ADAM_EPS = 0.001
SOFTEN = 0.01


def rotation(quaternion):
    length = jnp.sqrt(jnp.sum(quaternion * quaternion, axis=-1))
    w = quaternion[..., 0] / length
    x = quaternion[..., 1] / length
    y = quaternion[..., 2] / length
    z = quaternion[..., 3] / length
    return [
        [1.0 - 2.0 * (y * y + z * z), 2.0 * (x * y - w * z), 2.0 * (x * z + w * y)],
        [2.0 * (x * y + w * z), 1.0 - 2.0 * (x * x + z * z), 2.0 * (y * z - w * x)],
        [2.0 * (x * z - w * y), 2.0 * (y * z + w * x), 1.0 - 2.0 * (x * x + y * y)],
    ]


def world_points(log_depths, cameras):
    pixel_count = log_depths.shape[-1]
    position = jnp.arange(pixel_count, dtype=jnp.int32)
    across = (position % IMG_WIDTH).astype(jnp.float32) - (IMG_WIDTH - 1) / 2.0
    downward = (position // IMG_WIDTH + (IMG_HEIGHT - WIN_ROWS) // 2).astype(jnp.float32) - (
        IMG_HEIGHT - 1
    ) / 2.0
    focal_len = jnp.exp(cameras[:, 7:8])
    depth_map = jnp.exp(log_depths)
    ray_parts = (
        across[None, :] / focal_len * depth_map,
        downward[None, :] / focal_len * depth_map,
        depth_map,
    )
    turned = rotation(cameras[:, 0:4])
    return [
        turned[k][0][:, None] * ray_parts[0]
        + turned[k][1][:, None] * ray_parts[1]
        + turned[k][2][:, None] * ray_parts[2]
        + cameras[:, 4 + k][:, None]
        for k in range(3)
    ]


def pair_loss(
    first_depth,
    second_depth,
    first_camera,
    second_camera,
    pair_params,
    pointmaps,
    confidence,
    valid_blocks,
    first_ids,
    second_ids,
):
    first_world = world_points(first_depth, first_camera)
    second_world = world_points(second_depth, second_camera)
    pair_rotation = rotation(pair_params[..., 0:4])
    pair_scale = jnp.exp(pair_params[..., 7])
    pair_keep = (first_ids[:, None] != second_ids[None, :]).astype(jnp.float32)
    pixel_keep = (
        jnp.repeat(valid_blocks.astype(jnp.float32), IMG_WIDTH, axis=2) * pair_keep[:, :, None]
    )
    loss_sum = jnp.zeros((), jnp.float32)
    for side_index in range(2):
        if side_index == 0:
            points_side = [first_world[k][:, None, :] for k in range(3)]
        else:
            points_side = [second_world[k][None, :, :] for k in range(3)]
        source = [pointmaps[:, :, side_index, k, :].astype(jnp.float32) for k in range(3)]
        squared = SOFTEN
        for k in range(3):
            aligned = (
                pair_scale[..., None]
                * (
                    pair_rotation[k][0][..., None] * source[0]
                    + pair_rotation[k][1][..., None] * source[1]
                    + pair_rotation[k][2][..., None] * source[2]
                )
                + pair_params[..., 4 + k][..., None]
            )
            residual = points_side[k] - aligned
            squared = squared + residual * residual
        weight = confidence[:, :, side_index, :].astype(jnp.float32) * pixel_keep
        loss_sum = loss_sum + jnp.sum(weight * jnp.sqrt(squared))
    return loss_sum / (2.0 * (IMAGES - 1))


def adam_step(param, grad, first, second, step_number, step_size):
    first = BETA_ONE * first + (1.0 - BETA_ONE) * grad
    second = BETA_TWO * second + (1.0 - BETA_TWO) * grad * grad
    update = (
        step_size
        * (first / (1.0 - BETA_ONE**step_number))
        / (jnp.sqrt(second / (1.0 - BETA_TWO**step_number)) + ADAM_EPS)
    )
    return (param - update, first, second)


def body(pointmaps, confidence, valid_blocks, log_depth, camera, pair_pose, step_sizes):
    row_count = pointmaps.shape[0]
    col_count = pointmaps.shape[1]
    row_index = lax.axis_index("row")
    col_index = lax.axis_index("col")
    first_ids = row_index * row_count + jnp.arange(row_count, dtype=jnp.int32)
    second_ids = col_index * col_count + jnp.arange(col_count, dtype=jnp.int32)

    def local_loss(row_depth, col_depth, cameras, pair_params):
        first_camera = lax.dynamic_slice_in_dim(cameras, row_index * row_count, row_count, 0)
        second_camera = lax.dynamic_slice_in_dim(cameras, col_index * col_count, col_count, 0)
        return pair_loss(
            row_depth,
            col_depth,
            first_camera,
            second_camera,
            pair_params,
            pointmaps,
            confidence,
            valid_blocks,
            first_ids,
            second_ids,
        )

    depth_now, camera_now, pair_now = (log_depth, camera, pair_pose)
    depth_first = jnp.zeros_like(log_depth)
    depth_second = jnp.zeros_like(log_depth)
    camera_first = jnp.zeros_like(camera)
    camera_second = jnp.zeros_like(camera)
    pair_first = jnp.zeros_like(pair_pose)
    pair_second = jnp.zeros_like(pair_pose)
    for step_number in range(1, ADAM_STEPS + 1):
        row_depth = lax.all_gather(depth_now, "col", axis=1, tiled=True)
        every_image = lax.all_gather(depth_now, "row", axis=0, tiled=True)
        col_depth = lax.all_to_all(every_image, "col", split_axis=0, concat_axis=1, tiled=True)
        row_grad, col_grad, cam_grad, pair_grad = jax.grad(local_loss, argnums=(0, 1, 2, 3))(
            row_depth, col_depth, camera_now, pair_now
        )
        returned = lax.all_to_all(col_grad, "col", split_axis=1, concat_axis=0, tiled=True)
        from_cols = lax.psum_scatter(returned, "row", scatter_dimension=0, tiled=True)
        depth_grad = lax.psum_scatter(row_grad, "col", scatter_dimension=1, tiled=True)
        depth_grad = depth_grad + from_cols
        cam_total = lax.psum(cam_grad, ("row", "col"))
        depth_now, depth_first, depth_second = adam_step(
            depth_now, depth_grad, depth_first, depth_second, step_number, step_sizes[0]
        )
        camera_now, camera_first, camera_second = adam_step(
            camera_now, cam_total, camera_first, camera_second, step_number, step_sizes[1]
        )
        pair_now, pair_first, pair_second = adam_step(
            pair_now, pair_grad, pair_first, pair_second, step_number, step_sizes[2]
        )
    return (depth_now, camera_now, pair_now)


def solution(mesh):
    in_specs = (
        P("row", "col", None, None, None),
        P("row", "col", None, None),
        P("row", "col", None),
        P("row", "col"),
        P(),
        P("row", "col", None),
        P(),
    )
    out_specs = (P("row", "col"), P(), P("row", "col", None))
    return jax.shard_map(body, mesh=mesh, in_specs=in_specs, out_specs=out_specs, check_vma=False)
```

profile of v0, /device:TPU:10, one launch (start us, length us, event | category | flops | bytes accessed | tf_op | source)
XLA Modules:
  0.0 630.6 jit_solution(9990873873530797576)
XLA Ops:
  7.2 10.4 %all_gather.13 = f32[64,1792]{1,0:T(8,128)} all-gather(f32[16,1792]{1,0:T(8,128)} %param.10), channel_id=1, replica_groups=mesh['row'=4,'col'=8] {'row'}, dimensions={0}, use_global_device_ids=true | all-gather | bytes 573440 | tf_op jit(solution)/shard_map/all_gather | solution.py:143
  17.6 5.3 all-to-all-start
  23.0 23.3 %all_gather.12 = f32[16,14336]{1,0:T(8,128)S(1)} all-gather(f32[16,1792]{1,0:T(8,128)} %param.10), channel_id=1, replica_groups=mesh['row'=4,'col'=8] {'col'}, dimensions={1}, use_global_device_ids=true | all-gather | bytes 1032192 | tf_op jit(solution)/shard_map/all_gather | solution.py:142
  48.8 60.3 %fusion.394 = (bf16[16,8,1,1,14336]{4,2,3,1,0:T(2,128)(2,1)}, bf16[16,8,1,1,14336]{4,2,3,1,0:T(2,128)(2,1)}, bf16[16,8,1,1,14336]{4,2,3,1,0:T(2,128)(2,1)}, bf16...) fusion(bf16[16,8,2,3,14336]{4,2,3,1,0:T(2,128)(2,1)} %param.7), kind=kLoop, calls=%fused_computation.1094 | loop fusion | bytes 44040192 | tf_op jit(solution)/shard_map/jvp()/slice | solution.py:80
  109.1 3.8 broadcast_in_dim.14
  113.0 9.5 %reshape.2729 = f32[16,8,14336]{2,1,0:T(8,128)} reshape(f32[16,8,64,224]{3,2,1,0:T(8,128)} %broadcast_in_dim.14) | data formatting | bytes 14680064 | tf_op jit(solution)/shard_map/jvp()/reshape | solution.py:72
  122.5 17.9 %fusion.395 = (bf16[16,8,1,14336]{3,2,1,0:T(2,128)(2,1)}, bf16[16,8,1,14336]{3,2,1,0:T(2,128)(2,1)}) fusion(bf16[16,8,2,14336]{3,2,1,0:T(2,128)(2,1)} %param.8), kind=kLoop, calls=%fused_computation.1095 | loop fusion | bytes 14680064 | tf_op jit(solution)/shard_map/jvp()/slice | solution.py:94
  143.4 25.0 %add_multiply_fusion.9 = (f32[16,8,14336]{2,1,0:T(8,128)}, f32[16,8,14336]{2,1,0:T(8,128)}, bf16[16,8,14336]{2,1,0:T(8,128)(2,1)S(1)}, bf16[16,8,14336]{2,1,0:T(8,128)(2,1)}, bf16[16,8,14336]{2,1,0:T(8,128)(2,1)}) fusion(f32[16,8]{1,0:T(8,128)S(1)} %copy.311, f32[16,14336]{1,0:T(8,128)} %get-tuple-element.230, f32[16,8]{1,0:T(8,128)S(1)} %copy.292, ...), kind=kLoop, calls=%fused_computation.145 | loop fusion | flops 75235328 | bytes 50469888 | tf_op jit(solution)/shard_map/transpose(jvp())/add_any | solution.py:93
  168.5 14.6 %add_multiply_fusion.10 = (f32[16,8,14336]{2,1,0:T(8,128)}, f32[16,8,14336]{2,1,0:T(8,128)}) fusion(f32[16,8,14336]{2,1,0:T(8,128)} %get-tuple-element.191, f32[16,8]{1,0:T(8,128)S(1)} %copy.316, f32[16,14336]{1,0:T(8,128)S(1)} %get-tuple-element.229, f32[16,8]{1,0:T(8,128)S(1)} %copy.292, bf16[16,8,14336]{2,1,0:T(8,128)(2,1)} %get-tuple-element.194, ...), kind=kLoop, calls=%fused_computation.146 | loop fusion | flops 42205184 | bytes 34869760 | tf_op jit(solution)/shard_map/transpose(jvp())/add_any | solution.py:93
  183.1 31.7 %multiply_reduce_fusion.8 = (f32[16,8]{1,0:T(8,128)S(1)}, f32[16,8]{1,0:T(8,128)S(1)}, f32[16,8]{1,0:T(8,128)S(1)}, f32[16,8]{1,0:T(8,128)S(1)}, f32[16,8]{1,0:T...) fusion(f32[16,8,14336]{2,1,0:T(8,128)} %get-tuple-element.219, ...), kind=kLoop, calls=%fused_computation.164 | loop fusion | flops 103905360 | bytes 35795648 | tf_op jit(solution)/shard_map/transpose(jvp())/reduce_sum | solution.py:84
  214.9 3.5 multiply_reduce_fusion.24
  226.6 24.6 %add_multiply_fusion.8 = (f32[16,8,14336]{2,1,0:T(8,128)}, f32[16,8,14336]{2,1,0:T(8,128)}, bf16[16,8,14336]{2,1,0:T(8,128)(2,1)S(1)}, bf16[16,8,14336]{2,1,0:T(8,128)(2,1)S(1)}, bf16[16,8,14336]{2,1,0:T(8,128)(2,1)S(1)}) fusion(f32[8,14336]{1,0:T(8,128)S(1)} %get-tuple-element.236, f32[16,8]{1,0:T(8,128)S(1)} %copy.305, f32[16,8]{1,0:T(8,128)S(1)} %copy.292, ...), kind=kLoop, calls=%fused_computation.144 | loop fusion | flops 75235328 | bytes 49093632 | tf_op jit(solution)/shard_map/transpose(jvp())/add_any | solution.py:93
  251.2 13.2 %add_multiply_fusion.6 = (f32[16,8,14336]{2,1,0:T(8,128)S(1)}, f32[16,8,14336]{2,1,0:T(8,128)}) fusion(f32[16,8,14336]{2,1,0:T(8,128)} %get-tuple-element.181, f32[8,14336]{1,0:T(8,128)S(1)} %get-tuple-element.235, f32[16,8]{1,0:T(8,128)S(1)} %copy.311, f32[16,8]{1,0:T(8,128)S(1)} %copy.292, bf16[16,8,14336]{2,1,0:T(8,128)(2,1)S(1)} %get-tuple-element.184, ...), kind=kLoop, calls=%fused_computation.142 | loop fusion | flops 42205184 | bytes 33952256 | tf_op jit(solution)/shard_map/transpose(jvp())/add_any | solution.py:93
  264.5 31.6 %multiply_reduce_fusion.10 = (f32[16,8]{1,0:T(8,128)S(1)}, f32[16,8]{1,0:T(8,128)S(1)}, f32[16,8]{1,0:T(8,128)S(1)}, f32[16,8]{1,0:T(8,128)S(1)}, f32[16,8]{1,0:...) fusion(f32[16,8,14336]{2,1,0:T(8,128)} %get-tuple-element.217, ...), kind=kLoop, calls=%fused_computation.166 | loop fusion | flops 104249448 | bytes 34419296 | tf_op jit(solution)/shard_map/transpose(jvp())/reduce_sum | solution.py:84
  299.5 41.0 %psum.14 = f32[64,8]{0,1:T(8,128)S(1)} all-reduce(f32[64,8]{0,1:T(8,128)S(1)} %add_any.2152), channel_id=1, replica_groups=mesh['row'=4,'col'=8] {'row','col'}, use_global_device_ids=true, to_apply=%region_39.40 | all-reduce | flops 512 | bytes 4096 | tf_op jit(solution)/shard_map/psum | solution.py:152
  341.1 4.1 all-to-all-start.1
  347.2 9.1 %all-to-all-done.1 = f32[8,8,1792]{2,0,1:T(8,128)S(1)} async-done(((f32[8,8,1792]{2,0,1:T(8,128)}), f32[8,8,1792]{2,0,1:T(8,128)S(1)}, u32[]{:S(2)}, u32[]{:S(2)}) %all-to-all-start.1) | async-done | bytes 458784 | tf_op jit(solution)/shard_map/all_to_all | solution.py:148
  358.8 23.6 %reduce-scatter.7.cloned.1.call-done = f32[16,1792]{1,0:T(8,128)} async-done(((f32[64,1792]{1,0:T(8,128)}), f32[16,1792]{1,0:T(8,128)}) %reduce-scatter.7.cloned.1.call-update) | async-done | bytes 114704 | tf_op jit(solution)/shard_map/reduce_scatter | solution.py:149
  384.4 9.5 %all_gather.15 = f32[64,1792]{1,0:T(8,128)} all-gather(f32[16,1792]{1,0:T(8,128)S(1)} %divide_subtract_fusion), channel_id=1, replica_groups=mesh['row'=4,'col'=8] {'row'}, dimensions={0}, use_global_device_ids=true | all-gather | bytes 573440 | tf_op jit(solution)/shard_map/all_gather | solution.py:143
  394.0 16.0 %all_gather.14 = f32[16,14336]{1,0:T(8,128)S(1)} all-gather(f32[16,1792]{1,0:T(8,128)S(1)} %divide_subtract_fusion), channel_id=1, replica_groups=mesh['row'=4,'col'=8] {'col'}, dimensions={1}, use_global_device_ids=true | all-gather | bytes 1032192 | tf_op jit(solution)/shard_map/all_gather | solution.py:142
  410.8 17.8 %add_multiply_fusion.3 = (f32[16,8,14336]{2,1,0:T(8,128)}, f32[16,8,14336]{2,1,0:T(8,128)}) fusion(f32[16,8]{1,0:T(8,128)S(1)} %copy.355, f32[16,14336]{1,0:T(8,128)S(1)} %get-tuple-element.227, f32[16,8]{1,0:T(8,128)S(1)} %copy.347, bf16[16,8,14336]{2,1,0:T(8,128)(2,1)} %get-tuple-element.194, f32[16,8]{1,0:T(8,128)S(1)} %copy.354, ...), kind=kLoop, calls=%fused_computation.139 | loop fusion | flops 75235328 | bytes 39459840 | tf_op jit(solution)/shard_map/transpose(jvp())/add_any | solution.py:93
  428.6 11.2 %add_multiply_fusion.4 = (f32[16,8,14336]{2,1,0:T(8,128)}, f32[16,8,14336]{2,1,0:T(8,128)}) fusion(f32[16,8,14336]{2,1,0:T(8,128)} %get-tuple-element.161, f32[16,8]{1,0:T(8,128)S(1)} %copy.359, f32[16,14336]{1,0:T(8,128)S(1)} %get-tuple-element.226, f32[16,8]{1,0:T(8,128)S(1)} %copy.347, bf16[16,8,14336]{2,1,0:T(8,128)(2,1)S(1)} %copy-done.6, ...), kind=kLoop, calls=%fused_computation.140 | loop fusion | flops 42205184 | bytes 34869760 | tf_op jit(solution)/shard_map/transpose(jvp())/add_any | solution.py:93
  439.8 31.5 %multiply_reduce_fusion.2 = (f32[16,8]{1,0:T(8,128)S(1)}, f32[16,8]{1,0:T(8,128)}, f32[16,8]{1,0:T(8,128)S(1)}, f32[16,8]{1,0:T(8,128)S(1)}, f32[16,8]{1,0:T(8,1...) fusion(f32[16,8,14336]{2,1,0:T(8,128)} %get-tuple-element.215, ...), kind=kLoop, calls=%fused_computation.150 | loop fusion | flops 103905360 | bytes 35795648 | tf_op jit(solution)/shard_map/transpose(jvp())/reduce_sum | solution.py:84
  471.4 2.9 multiply_reduce_fusion.13
  474.3 5.3 all-to-all-start.2
  486.3 4.4 all-to-all-done.2
  491.3 20.2 %add_multiply_fusion = (f32[16,8,14336]{2,1,0:T(8,128)}, f32[16,8,14336]{2,1,0:T(8,128)}) fusion(f32[8,14336]{1,0:T(8,128)S(1)} %get-tuple-element.234, f32[16,8]{1,0:T(8,128)S(1)} %copy.355, f32[16,8]{1,0:T(8,128)S(1)} %copy.347, bf16[16,8,14336]{2,1,0:T(8,128)(2,1)} %copy-done.11, f32[16,8]{1,0:T(8,128)S(1)} %copy.354, ...), kind=kLoop, calls=%fused_computation.136 | loop fusion | flops 75235328 | bytes 38083584 | tf_op jit(solution)/shard_map/transpose(jvp())/add_any | solution.py:93
  511.5 10.4 %add_multiply_fusion.2 = (f32[16,8,14336]{2,1,0:T(8,128)S(1)}, f32[16,8,14336]{2,1,0:T(8,128)}) fusion(f32[16,8,14336]{2,1,0:T(8,128)} %get-tuple-element.154, f32[8,14336]{1,0:T(8,128)S(1)} %get-tuple-element.233, f32[16,8]{1,0:T(8,128)S(1)} %copy.351, f32[16,8]{1,0:T(8,128)S(1)} %copy.347, bf16[16,8,14336]{2,1,0:T(8,128)(2,1)S(1)} %copy-done.12, ...), kind=kLoop, calls=%fused_computation.138 | loop fusion | flops 42205184 | bytes 33952256 | tf_op jit(solution)/shard_map/transpose(jvp())/add_any | solution.py:93
  521.9 32.2 %multiply_reduce_fusion.4 = (f32[16,8]{1,0:T(8,128)S(1)}, f32[16,8]{1,0:T(8,128)S(1)}, f32[16,8]{1,0:T(8,128)S(1)}, f32[16,8]{1,0:T(8,128)S(1)}, f32[16,8]{1,0:T...) fusion(f32[16,8,14336]{2,1,0:T(8,128)} %get-tuple-element.213, ...), kind=kLoop, calls=%fused_computation.152 | loop fusion | flops 104249448 | bytes 34419296 | tf_op jit(solution)/shard_map/transpose(jvp())/reduce_sum | solution.py:84
  557.7 6.3 all-to-all-start.3
  566.2 8.8 %all-to-all-done.3 = f32[8,8,1792]{2,0,1:T(8,128)S(1)} async-done(((f32[8,8,1792]{2,0,1:T(8,128)}), f32[8,8,1792]{2,0,1:T(8,128)S(1)}, u32[]{:S(2)}, u32[]{:S(2)}) %all-to-all-start.3) | async-done | bytes 458784 | tf_op jit(solution)/shard_map/all_to_all | solution.py:148
  579.1 42.3 %psum.15 = f32[64,8]{0,1:T(8,128)S(1)} all-reduce(f32[64,8]{0,1:T(8,128)S(1)} %add_any.2425), channel_id=1, replica_groups=mesh['row'=4,'col'=8] {'row','col'}, use_global_device_ids=true, to_apply=%region_109.110 | all-reduce | flops 512 | bytes 4096 | tf_op jit(solution)/shard_map/psum | solution.py:152
  (305 shorter events, 42.3 us)
Async XLA Ops:
  17.6 208.5 %all-to-all-start = ((f32[8,8,1792]{2,1,0:T(8,128)}), f32[8,8,1792]{2,1,0:T(8,128)S(1)}, u32[]{:S(2)}, u32[]{:S(2)}) async-start(f32[8,8,1792]{2,1,0:T(8,128)} %bitcast.39), calls=%async_computation.1 | async-start | bytes 917504 | tf_op jit(solution)/shard_map/all_to_all | solution.py:144
  22.9 335.9 %reduce-scatter.5.cloned.1.call-start = ((), (), s32[]{:S(2)}) async-start(), calls=%async_computation.8 | async-start | bytes 1032192 | tf_op jit(solution)/shard_map/reduce_scatter | solution.py:150
  47.1 93.9 %copy-start.26 = (f32[16,1]{0,1:T(1,128)}, f32[16,1]{0,1:T(1,128)S(1)}, u32[]{:S(2)}) copy-start(f32[16,1]{0,1:T(1,128)S(1)} %get-tuple-element.202) | copy-start | bytes 196
  47.1 94.6 %copy-start.39 = (f32[16]{0:T(128)}, f32[16]{0:T(128)S(1)}, u32[]{:S(2)}) copy-start(f32[16]{0:T(128)S(1)} %get-tuple-element.200) | copy-start | bytes 196
  48.8 60.3 %copy-start.19 = (s32[16,8,64]{2,1,0:T(8,128)S(1)}, s32[16,8,64]{2,1,0:T(8,128)}, u32[]{:S(2)}) copy-start(s32[16,8,64]{2,1,0:T(8,128)} %param.9) | copy-start | bytes 98308
  264.4 80.8 %copy-start.21 = (f32[16,8]{1,0:T(8,128)S(1)}, f32[16,8]{1,0:T(8,128)}, u32[]{:S(2)}) copy-start(f32[16,8]{1,0:T(8,128)} %get-tuple-element.62) | copy-start | bytes 1540
  264.4 82.0 %copy-start.18 = (f32[16,8,8]{0,2,1:T(8,128)S(1)}, f32[16,8,8]{0,2,1:T(8,128)}, u32[]{:S(2)}) copy-start(f32[16,8,8]{0,2,1:T(8,128)} %param.12) | copy-start | bytes 12292
  264.5 118.0 %copy-start.15 = (f32[16,1792]{1,0:T(8,128)S(1)}, f32[16,1792]{1,0:T(8,128)}, u32[]{:S(2)}) copy-start(f32[16,1792]{1,0:T(8,128)} %param.10) | copy-start | bytes 344068
  341.1 15.2 %all-to-all-start.1 = ((f32[8,8,1792]{2,0,1:T(8,128)}), f32[8,8,1792]{2,0,1:T(8,128)S(1)}, u32[]{:S(2)}, u32[]{:S(2)}) async-start(f32[8,8,1792]{2,0,1:T(8,128)} %get-tuple-element.225), calls=%async_computation.2 | async-start | bytes 917504 | tf_op jit(solution)/shard_map/all_to_all | solution.py:148
  345.3 37.2 %reduce-scatter.7.cloned.1.call-start = ((), (), s32[]{:S(2)}) async-start(), calls=%async_computation.9 | async-start | bytes 573440 | tf_op jit(solution)/shard_map/reduce_scatter | solution.py:149
  357.1 71.4 %copy-start.28 = (f32[8]{0:T(128)}, f32[8]{0:T(128)S(1)}, u32[]{:S(2)}) copy-start(f32[8]{0:T(128)S(1)} %multiply_reduce_fusion.48) | copy-start | bytes 100
  358.6 69.9 %copy-start.49 = (f32[8,1]{0,1:T(1,128)}, f32[8,1]{0,1:T(1,128)S(1)}, u32[]{:S(2)}) copy-start(f32[8,1]{0,1:T(1,128)S(1)} %get-tuple-element.310) | copy-start | bytes 100
  358.6 69.9 %copy-start.50 = (f32[8,1]{0,1:T(1,128)}, f32[8,1]{0,1:T(1,128)S(1)}, u32[]{:S(2)}) copy-start(f32[8,1]{0,1:T(1,128)S(1)} %get-tuple-element.311) | copy-start | bytes 100
  358.6 69.9 %copy-start.51 = (f32[8,1]{0,1:T(1,128)}, f32[8,1]{0,1:T(1,128)S(1)}, u32[]{:S(2)}) copy-start(f32[8,1]{0,1:T(1,128)S(1)} %get-tuple-element.312) | copy-start | bytes 100
  358.6 69.9 %copy-start.52 = (f32[8,1]{0,1:T(1,128)}, f32[8,1]{0,1:T(1,128)S(1)}, u32[]{:S(2)}) copy-start(f32[8,1]{0,1:T(1,128)S(1)} %get-tuple-element.313) | copy-start | bytes 100
  358.7 132.1 %copy-start.29 = (f32[8]{0:T(128)}, f32[8]{0:T(128)S(1)}, u32[]{:S(2)}) copy-start(f32[8]{0:T(128)S(1)} %get-tuple-element.308) | copy-start | bytes 100
  358.7 132.1 %copy-start.30 = (f32[8]{0:T(128)}, f32[8]{0:T(128)S(1)}, u32[]{:S(2)}) copy-start(f32[8]{0:T(128)S(1)} %get-tuple-element.309) | copy-start | bytes 100
  358.7 132.0 %copy-start.31 = (f32[8]{0:T(128)}, f32[8]{0:T(128)S(1)}, u32[]{:S(2)}) copy-start(f32[8]{0:T(128)S(1)} %get-tuple-element.332) | copy-start | bytes 100
  358.7 132.0 %copy-start.32 = (f32[8]{0:T(128)}, f32[8]{0:T(128)S(1)}, u32[]{:S(2)}) copy-start(f32[8]{0:T(128)S(1)} %get-tuple-element.333) | copy-start | bytes 100
  358.7 132.0 %copy-start.33 = (f32[8]{0:T(128)}, f32[8]{0:T(128)S(1)}, u32[]{:S(2)}) copy-start(f32[8]{0:T(128)S(1)} %get-tuple-element.334) | copy-start | bytes 100
  358.7 132.0 %copy-start.34 = (f32[8]{0:T(128)}, f32[8]{0:T(128)S(1)}, u32[]{:S(2)}) copy-start(f32[8]{0:T(128)S(1)} %get-tuple-element.335) | copy-start | bytes 100
  358.7 132.0 %copy-start.35 = (f32[8]{0:T(128)}, f32[8]{0:T(128)S(1)}, u32[]{:S(2)}) copy-start(f32[8]{0:T(128)S(1)} %get-tuple-element.336) | copy-start | bytes 100
  358.7 132.0 %copy-start.36 = (f32[8]{0:T(128)}, f32[8]{0:T(128)S(1)}, u32[]{:S(2)}) copy-start(f32[8]{0:T(128)S(1)} %get-tuple-element.352) | copy-start | bytes 100
  358.8 132.0 %copy-start.37 = (f32[8]{0:T(128)}, f32[8]{0:T(128)S(1)}, u32[]{:S(2)}) copy-start(f32[8]{0:T(128)S(1)} %get-tuple-element.353) | copy-start | bytes 100
  358.8 132.0 %copy-start.38 = (f32[8]{0:T(128)}, f32[8]{0:T(128)S(1)}, u32[]{:S(2)}) copy-start(f32[8]{0:T(128)S(1)} %get-tuple-element.354) | copy-start | bytes 100
  474.3 16.3 %all-to-all-start.2 = ((f32[8,8,1792]{2,1,0:T(8,128)}), f32[8,8,1792]{2,1,0:T(8,128)S(1)}, u32[]{:S(2)}, u32[]{:S(2)}) async-start(f32[8,8,1792]{2,1,0:T(8,128)} %bitcast.156), calls=%async_computation.5 | async-start | bytes 917504 | tf_op jit(solution)/shard_map/all_to_all | solution.py:144
  479.6 142.4 %reduce-scatter.9.cloned.1.call-start = ((), (), s32[]{:S(2)}) async-start(), calls=%async_computation.10 | async-start | bytes 1032192 | tf_op jit(solution)/shard_map/reduce_scatter | solution.py:150
  521.9 42.8 %copy-start.25 = (f32[16,8]{0,1:T(8,128)S(1)}, f32[16,8]{0,1:T(8,128)}, u32[]{:S(2)}) copy-start(f32[16,8]{0,1:T(8,128)} %copy.372) | copy-start | bytes 1540
  521.9 100.1 %copy-start.16 = (f32[16,1792]{1,0:T(8,128)S(1)}, f32[16,1792]{1,0:T(8,128)}, u32[]{:S(2)}) copy-start(f32[16,1792]{1,0:T(8,128)} %reduce-scatter.5.cloned.1.call-done) | copy-start | bytes 344068
  521.9 100.1 %copy-start.17 = (f32[16,1792]{1,0:T(8,128)S(1)}, f32[16,1792]{1,0:T(8,128)}, u32[]{:S(2)}) copy-start(f32[16,1792]{1,0:T(8,128)} %reduce-scatter.7.cloned.1.call-done) | copy-start | bytes 344068
  557.7 17.3 %all-to-all-start.3 = ((f32[8,8,1792]{2,0,1:T(8,128)}), f32[8,8,1792]{2,0,1:T(8,128)S(1)}, u32[]{:S(2)}, u32[]{:S(2)}) async-start(f32[8,8,1792]{2,0,1:T(8,128)} %get-tuple-element.224), calls=%async_computation.6 | async-start | bytes 917504 | tf_op jit(solution)/shard_map/all_to_all | solution.py:148
  563.9 58.1 %reduce-scatter.11.cloned.1.call-start = ((), (), s32[]{:S(2)}) async-start(), calls=%async_computation.11 | async-start | bytes 573440 | tf_op jit(solution)/shard_map/reduce_scatter | solution.py:149
  (37 other events, 845.2 us)
Sparse Core Ops, SparseCore 0:
  218.5 29.3 reduce-scatter.4
  357.2 25.1 reduce-scatter.6
  483.5 29.3 reduce-scatter.8
  575.9 26.0 reduce-scatter.10
where the time goes:
time: 641 us; the launch traced here: 631 us
  other arithmetic  297 us (46%)
  blocking collectives  143 us (22%)
  local copies, waits for them, and re-layouts  107 us (17%)
  waiting for transfers between devices  46 us (7%)
  starting transfers between devices  21 us (3%)
  between operations  17 us (3%)
    add_any x8, other arithmetic, pair_loss(): squared = squared + residual * residual  137 us
    reduce_sum x4, other arithmetic, pair_loss(): pair_scale[..., None]  127 us
    psum x2, blocking collectives, body(): cam_total = lax.psum(cam_grad, ('row', 'col'))  83.3 us
    slice x1, local copies, waits for them, and re-layouts, pair_loss(): pointmaps[:, :, side_index, k, :].astype(jnp.float32)  60.3 us
    all_gather x2, blocking collectives, body(): row_depth = lax.all_gather(depth_now, 'col', axis=1, tiled=True)  39.3 us
    reduce_scatter x2, waiting for transfers between devices, body(): lax.psum_scatter(returned, 'row', scatter_dimension=0, tiled=True)  23.6 us
    all_gather x2, blocking collectives, body(): every_image = lax.all_gather(depth_now, 'row', axis=0, tiled=True)  20 us
    slice x1, local copies, waits for them, and re-layouts, pair_loss(): weight = confidence[:, :, side_index, :].astype(jnp.float32) * pixel_keep  17.9 us
  transfers between devices with their start and end apart: 8, of which 4 were waited for; matrix products, arithmetic and copies ran while one was open for 53% of the time, Pallas kernels for 0%

commit v1 on v0

--- a/solution.py
+++ b/solution.py
@@ -149,7 +149,9 @@
         from_cols = lax.psum_scatter(returned, "row", scatter_dimension=0, tiled=True)
         depth_grad = lax.psum_scatter(row_grad, "col", scatter_dimension=1, tiled=True)
         depth_grad = depth_grad + from_cols
-        cam_total = lax.psum(cam_grad, ("row", "col"))
+        cam_total = cam_grad
+        for dd in ("col", "row"):
+            cam_total = lax.psum(cam_total, axis_name=dd)
         depth_now, depth_first, depth_second = adam_step(
             depth_now, depth_grad, depth_first, depth_second, step_number, step_sizes[0]
         )

time: 641 us -> 612 us (0.955)
  the two profiles are of different devices: /device:TPU:10 before, /device:TPU:0 now
where the time goes in v1:
time: 612 us; the launch traced here: 601 us
  other arithmetic  297 us (49%)
  blocking collectives  113 us (18%)
  local copies, waits for them, and re-layouts  107 us (17%)
  waiting for transfers between devices  51.2 us (8%)
  between operations  16.9 us (3%)
  starting transfers between devices  16.1 us (3%)
    add_any x8, other arithmetic, pair_loss(): squared = squared + residual * residual  137 us
    reduce_sum x4, other arithmetic, pair_loss(): pair_scale[..., None]  127 us
    slice x1, local copies, waits for them, and re-layouts, pair_loss(): pointmaps[:, :, side_index, k, :].astype(jnp.float32)  60.3 us
    psum x4, blocking collectives, body(): cam_total = lax.psum(cam_total, axis_name=dd)  49.6 us
    all_gather x2, blocking collectives, body(): row_depth = lax.all_gather(depth_now, 'col', axis=1, tiled=True)  40 us
    all_to_all x2, waiting for transfers between devices, body(): lax.all_to_all(col_grad, 'col', split_axis=1, concat_axis=0, tiled=True)  23.3 us
    all_gather x2, blocking collectives, body(): every_image = lax.all_gather(depth_now, 'row', axis=0, tiled=True)  23.3 us
    reduce_scatter x2, waiting for transfers between devices, body(): lax.psum_scatter(returned, 'row', scatter_dimension=0, tiled=True)  20.4 us
  transfers between devices with their start and end apart: 8, of which 4 were waited for; matrix products, arithmetic and copies ran while one was open for 55% of the time, Pallas kernels for 0%

profile of v1, /device:TPU:0, one launch (start us, length us, event | category | flops | bytes accessed | tf_op | source)
XLA Modules:
  0.0 601.3 jit_solution(2599728377569439690)
XLA Ops:
  7.2 12.9 %all_gather.13 = f32[64,1792]{1,0:T(8,128)} all-gather(f32[16,1792]{1,0:T(8,128)} %param.10), channel_id=1, replica_groups=mesh['row'=4,'col'=8] {'row'}, dimensions={0}, use_global_device_ids=true | all-gather | bytes 573440 | tf_op jit(solution)/shard_map/all_gather | solution.py:143
  20.1 4.9 all-to-all-start
  25.0 23.4 %all_gather.12 = f32[16,14336]{1,0:T(8,128)S(1)} all-gather(f32[16,1792]{1,0:T(8,128)} %param.10), channel_id=1, replica_groups=mesh['row'=4,'col'=8] {'col'}, dimensions={1}, use_global_device_ids=true | all-gather | bytes 1032192 | tf_op jit(solution)/shard_map/all_gather | solution.py:142
  51.0 60.3 %fusion.394 = (bf16[16,8,1,1,14336]{4,2,3,1,0:T(2,128)(2,1)}, bf16[16,8,1,1,14336]{4,2,3,1,0:T(2,128)(2,1)}, bf16[16,8,1,1,14336]{4,2,3,1,0:T(2,128)(2,1)}, bf16...) fusion(bf16[16,8,2,3,14336]{4,2,3,1,0:T(2,128)(2,1)} %param.7), kind=kLoop, calls=%fused_computation.1094 | loop fusion | bytes 44040192 | tf_op jit(solution)/shard_map/jvp()/slice | solution.py:80
  111.3 3.8 broadcast_in_dim.14
  115.2 9.5 %reshape.2729 = f32[16,8,14336]{2,1,0:T(8,128)} reshape(f32[16,8,64,224]{3,2,1,0:T(8,128)} %broadcast_in_dim.14) | data formatting | bytes 14680064 | tf_op jit(solution)/shard_map/jvp()/reshape | solution.py:72
  124.7 17.9 %fusion.395 = (bf16[16,8,1,14336]{3,2,1,0:T(2,128)(2,1)}, bf16[16,8,1,14336]{3,2,1,0:T(2,128)(2,1)}) fusion(bf16[16,8,2,14336]{3,2,1,0:T(2,128)(2,1)} %param.8), kind=kLoop, calls=%fused_computation.1095 | loop fusion | bytes 14680064 | tf_op jit(solution)/shard_map/jvp()/slice | solution.py:94
  145.5 25.0 %add_multiply_fusion.9 = (f32[16,8,14336]{2,1,0:T(8,128)}, f32[16,8,14336]{2,1,0:T(8,128)}, bf16[16,8,14336]{2,1,0:T(8,128)(2,1)S(1)}, bf16[16,8,14336]{2,1,0:T(8,128)(2,1)}, bf16[16,8,14336]{2,1,0:T(8,128)(2,1)}) fusion(f32[16,8]{1,0:T(8,128)S(1)} %copy.311, f32[16,14336]{1,0:T(8,128)} %get-tuple-element.230, f32[16,8]{1,0:T(8,128)S(1)} %copy.292, ...), kind=kLoop, calls=%fused_computation.145 | loop fusion | flops 75235328 | bytes 50469888 | tf_op jit(solution)/shard_map/transpose(jvp())/add_any | solution.py:93
  170.6 14.9 %add_multiply_fusion.10 = (f32[16,8,14336]{2,1,0:T(8,128)}, f32[16,8,14336]{2,1,0:T(8,128)}) fusion(f32[16,8,14336]{2,1,0:T(8,128)} %get-tuple-element.191, f32[16,8]{1,0:T(8,128)S(1)} %copy.316, f32[16,14336]{1,0:T(8,128)S(1)} %get-tuple-element.229, f32[16,8]{1,0:T(8,128)S(1)} %copy.292, bf16[16,8,14336]{2,1,0:T(8,128)(2,1)} %get-tuple-element.194, ...), kind=kLoop, calls=%fused_computation.146 | loop fusion | flops 42205184 | bytes 34869760 | tf_op jit(solution)/shard_map/transpose(jvp())/add_any | solution.py:93
  185.6 31.7 %multiply_reduce_fusion.8 = (f32[16,8]{1,0:T(8,128)S(1)}, f32[16,8]{1,0:T(8,128)S(1)}, f32[16,8]{1,0:T(8,128)S(1)}, f32[16,8]{1,0:T(8,128)S(1)}, f32[16,8]{1,0:T...) fusion(f32[16,8,14336]{2,1,0:T(8,128)} %get-tuple-element.219, ...), kind=kLoop, calls=%fused_computation.164 | loop fusion | flops 103905360 | bytes 35795648 | tf_op jit(solution)/shard_map/transpose(jvp())/reduce_sum | solution.py:84
  229.0 24.4 %add_multiply_fusion.8 = (f32[16,8,14336]{2,1,0:T(8,128)}, f32[16,8,14336]{2,1,0:T(8,128)}, bf16[16,8,14336]{2,1,0:T(8,128)(2,1)S(1)}, bf16[16,8,14336]{2,1,0:T(8,128)(2,1)S(1)}, bf16[16,8,14336]{2,1,0:T(8,128)(2,1)S(1)}) fusion(f32[8,14336]{1,0:T(8,128)S(1)} %get-tuple-element.236, f32[16,8]{1,0:T(8,128)S(1)} %copy.305, f32[16,8]{1,0:T(8,128)S(1)} %copy.292, ...), kind=kLoop, calls=%fused_computation.144 | loop fusion | flops 75235328 | bytes 49093632 | tf_op jit(solution)/shard_map/transpose(jvp())/add_any | solution.py:93
  253.4 13.2 %add_multiply_fusion.6 = (f32[16,8,14336]{2,1,0:T(8,128)S(1)}, f32[16,8,14336]{2,1,0:T(8,128)}) fusion(f32[16,8,14336]{2,1,0:T(8,128)} %get-tuple-element.181, f32[8,14336]{1,0:T(8,128)S(1)} %get-tuple-element.235, f32[16,8]{1,0:T(8,128)S(1)} %copy.311, f32[16,8]{1,0:T(8,128)S(1)} %copy.292, bf16[16,8,14336]{2,1,0:T(8,128)(2,1)S(1)} %get-tuple-element.184, ...), kind=kLoop, calls=%fused_computation.142 | loop fusion | flops 42205184 | bytes 33952256 | tf_op jit(solution)/shard_map/transpose(jvp())/add_any | solution.py:93
  266.7 31.6 %multiply_reduce_fusion.10 = (f32[16,8]{1,0:T(8,128)S(1)}, f32[16,8]{1,0:T(8,128)S(1)}, f32[16,8]{1,0:T(8,128)S(1)}, f32[16,8]{1,0:T(8,128)S(1)}, f32[16,8]{1,0:...) fusion(f32[16,8,14336]{2,1,0:T(8,128)} %get-tuple-element.217, ...), kind=kLoop, calls=%fused_computation.166 | loop fusion | flops 104249448 | bytes 34419296 | tf_op jit(solution)/shard_map/transpose(jvp())/reduce_sum | solution.py:84
  301.6 17.2 %psum.28 = f32[64,8]{0,1:T(8,128)S(1)} all-reduce(f32[64,8]{0,1:T(8,128)S(1)} %add_any.2152), channel_id=1, replica_groups=mesh['row'=4,'col'=8] {'col'}, use_global_device_ids=true, to_apply=%region_39.40 | all-reduce | flops 512 | bytes 4096 | tf_op jit(solution)/shard_map/psum | solution.py:154
  318.7 9.0 %psum.29 = f32[64,8]{0,1:T(8,128)S(1)} all-reduce(f32[64,8]{0,1:T(8,128)S(1)} %psum.28), channel_id=1, replica_groups=mesh['row'=4,'col'=8] {'row'}, use_global_device_ids=true, to_apply=%region_40.41 | all-reduce | flops 512 | bytes 4096 | tf_op jit(solution)/shard_map/psum | solution.py:154
  328.4 3.5 all-to-all-start.1
  333.9 11.8 %all-to-all-done.1 = f32[8,8,1792]{2,0,1:T(8,128)S(1)} async-done(((f32[8,8,1792]{2,0,1:T(8,128)}), f32[8,8,1792]{2,0,1:T(8,128)S(1)}, u32[]{:S(2)}, u32[]{:S(2)}) %all-to-all-start.1) | async-done | bytes 458784 | tf_op jit(solution)/shard_map/all_to_all | solution.py:148
  348.3 20.4 %reduce-scatter.7.cloned.1.call-done = f32[16,1792]{1,0:T(8,128)} async-done(((f32[64,1792]{1,0:T(8,128)}), f32[16,1792]{1,0:T(8,128)}) %reduce-scatter.7.cloned.1.call-update) | async-done | bytes 114704 | tf_op jit(solution)/shard_map/reduce_scatter | solution.py:149
  370.6 10.4 %all_gather.15 = f32[64,1792]{1,0:T(8,128)} all-gather(f32[16,1792]{1,0:T(8,128)S(1)} %divide_subtract_fusion), channel_id=1, replica_groups=mesh['row'=4,'col'=8] {'row'}, dimensions={0}, use_global_device_ids=true | all-gather | bytes 573440 | tf_op jit(solution)/shard_map/all_gather | solution.py:143
  381.0 16.6 %all_gather.14 = f32[16,14336]{1,0:T(8,128)S(1)} all-gather(f32[16,1792]{1,0:T(8,128)S(1)} %divide_subtract_fusion), channel_id=1, replica_groups=mesh['row'=4,'col'=8] {'col'}, dimensions={1}, use_global_device_ids=true | all-gather | bytes 1032192 | tf_op jit(solution)/shard_map/all_gather | solution.py:142
  398.5 18.1 %add_multiply_fusion.3 = (f32[16,8,14336]{2,1,0:T(8,128)}, f32[16,8,14336]{2,1,0:T(8,128)}) fusion(f32[16,8]{1,0:T(8,128)S(1)} %copy.355, f32[16,14336]{1,0:T(8,128)S(1)} %get-tuple-element.227, f32[16,8]{1,0:T(8,128)S(1)} %copy.347, bf16[16,8,14336]{2,1,0:T(8,128)(2,1)} %get-tuple-element.194, f32[16,8]{1,0:T(8,128)S(1)} %copy.354, ...), kind=kLoop, calls=%fused_computation.139 | loop fusion | flops 75235328 | bytes 39459840 | tf_op jit(solution)/shard_map/transpose(jvp())/add_any | solution.py:93
  416.6 11.2 %add_multiply_fusion.4 = (f32[16,8,14336]{2,1,0:T(8,128)}, f32[16,8,14336]{2,1,0:T(8,128)}) fusion(f32[16,8,14336]{2,1,0:T(8,128)} %get-tuple-element.161, f32[16,8]{1,0:T(8,128)S(1)} %copy.359, f32[16,14336]{1,0:T(8,128)S(1)} %get-tuple-element.226, f32[16,8]{1,0:T(8,128)S(1)} %copy.347, bf16[16,8,14336]{2,1,0:T(8,128)(2,1)S(1)} %copy-done.6, ...), kind=kLoop, calls=%fused_computation.140 | loop fusion | flops 42205184 | bytes 34869760 | tf_op jit(solution)/shard_map/transpose(jvp())/add_any | solution.py:93
  427.8 31.5 %multiply_reduce_fusion.2 = (f32[16,8]{1,0:T(8,128)S(1)}, f32[16,8]{1,0:T(8,128)}, f32[16,8]{1,0:T(8,128)S(1)}, f32[16,8]{1,0:T(8,128)S(1)}, f32[16,8]{1,0:T(8,1...) fusion(f32[16,8,14336]{2,1,0:T(8,128)} %get-tuple-element.215, ...), kind=kLoop, calls=%fused_computation.150 | loop fusion | flops 103905360 | bytes 35795648 | tf_op jit(solution)/shard_map/transpose(jvp())/reduce_sum | solution.py:84
  462.3 4.1 all-to-all-start.2
  473.1 7.4 %all-to-all-done.2 = f32[8,8,1792]{2,1,0:T(8,128)S(1)} async-done(((f32[8,8,1792]{2,1,0:T(8,128)}), f32[8,8,1792]{2,1,0:T(8,128)S(1)}, u32[]{:S(2)}, u32[]{:S(2)}) %all-to-all-start.2) | async-done | bytes 458784 | tf_op jit(solution)/shard_map/all_to_all | solution.py:144
  481.1 20.2 %add_multiply_fusion = (f32[16,8,14336]{2,1,0:T(8,128)}, f32[16,8,14336]{2,1,0:T(8,128)}) fusion(f32[8,14336]{1,0:T(8,128)S(1)} %get-tuple-element.234, f32[16,8]{1,0:T(8,128)S(1)} %copy.355, f32[16,8]{1,0:T(8,128)S(1)} %copy.347, bf16[16,8,14336]{2,1,0:T(8,128)(2,1)} %copy-done.11, f32[16,8]{1,0:T(8,128)S(1)} %copy.354, ...), kind=kLoop, calls=%fused_computation.136 | loop fusion | flops 75235328 | bytes 38083584 | tf_op jit(solution)/shard_map/transpose(jvp())/add_any | solution.py:93
  501.4 10.4 %add_multiply_fusion.2 = (f32[16,8,14336]{2,1,0:T(8,128)S(1)}, f32[16,8,14336]{2,1,0:T(8,128)}) fusion(f32[16,8,14336]{2,1,0:T(8,128)} %get-tuple-element.154, f32[8,14336]{1,0:T(8,128)S(1)} %get-tuple-element.233, f32[16,8]{1,0:T(8,128)S(1)} %copy.351, f32[16,8]{1,0:T(8,128)S(1)} %copy.347, bf16[16,8,14336]{2,1,0:T(8,128)(2,1)S(1)} %copy-done.12, ...), kind=kLoop, calls=%fused_computation.138 | loop fusion | flops 42205184 | bytes 33952256 | tf_op jit(solution)/shard_map/transpose(jvp())/add_any | solution.py:93
  511.8 32.2 %multiply_reduce_fusion.4 = (f32[16,8]{1,0:T(8,128)S(1)}, f32[16,8]{1,0:T(8,128)S(1)}, f32[16,8]{1,0:T(8,128)S(1)}, f32[16,8]{1,0:T(8,128)S(1)}, f32[16,8]{1,0:T...) fusion(f32[16,8,14336]{2,1,0:T(8,128)} %get-tuple-element.213, ...), kind=kLoop, calls=%fused_computation.152 | loop fusion | flops 104249448 | bytes 34419296 | tf_op jit(solution)/shard_map/transpose(jvp())/reduce_sum | solution.py:84
  547.5 3.5 all-to-all-start.3
  553.4 11.5 %all-to-all-done.3 = f32[8,8,1792]{2,0,1:T(8,128)S(1)} async-done(((f32[8,8,1792]{2,0,1:T(8,128)}), f32[8,8,1792]{2,0,1:T(8,128)S(1)}, u32[]{:S(2)}, u32[]{:S(2)}) %all-to-all-start.3) | async-done | bytes 458784 | tf_op jit(solution)/shard_map/all_to_all | solution.py:148
  568.8 14.6 %psum.30 = f32[64,8]{0,1:T(8,128)S(1)} all-reduce(f32[64,8]{0,1:T(8,128)S(1)} %add_any.2425), channel_id=1, replica_groups=mesh['row'=4,'col'=8] {'col'}, use_global_device_ids=true, to_apply=%region_110.111 | all-reduce | flops 512 | bytes 4096 | tf_op jit(solution)/shard_map/psum | solution.py:154
  583.4 8.8 %psum.31 = f32[64,8]{0,1:T(8,128)S(1)} all-reduce(f32[64,8]{0,1:T(8,128)S(1)} %psum.30), channel_id=1, replica_groups=mesh['row'=4,'col'=8] {'row'}, use_global_device_ids=true, to_apply=%region_111.112 | all-reduce | flops 512 | bytes 4096 | tf_op jit(solution)/shard_map/psum | solution.py:154
  (307 shorter events, 48.5 us)
Async XLA Ops:
  20.1 208.5 %all-to-all-start = ((f32[8,8,1792]{2,1,0:T(8,128)}), f32[8,8,1792]{2,1,0:T(8,128)S(1)}, u32[]{:S(2)}, u32[]{:S(2)}) async-start(f32[8,8,1792]{2,1,0:T(8,128)} %bitcast.39), calls=%async_computation.1 | async-start | bytes 917504 | tf_op jit(solution)/shard_map/all_to_all | solution.py:144
  24.9 323.3 %reduce-scatter.5.cloned.1.call-start = ((), (), s32[]{:S(2)}) async-start(), calls=%async_computation.8 | async-start | bytes 1032192 | tf_op jit(solution)/shard_map/reduce_scatter | solution.py:150
  49.2 93.9 %copy-start.26 = (f32[16,1]{0,1:T(1,128)}, f32[16,1]{0,1:T(1,128)S(1)}, u32[]{:S(2)}) copy-start(f32[16,1]{0,1:T(1,128)S(1)} %get-tuple-element.202) | copy-start | bytes 196
  49.2 94.6 %copy-start.39 = (f32[16]{0:T(128)}, f32[16]{0:T(128)S(1)}, u32[]{:S(2)}) copy-start(f32[16]{0:T(128)S(1)} %get-tuple-element.200) | copy-start | bytes 196
  51.0 60.3 %copy-start.19 = (s32[16,8,64]{2,1,0:T(8,128)S(1)}, s32[16,8,64]{2,1,0:T(8,128)}, u32[]{:S(2)}) copy-start(s32[16,8,64]{2,1,0:T(8,128)} %param.9) | copy-start | bytes 98308
  266.6 65.3 %copy-start.21 = (f32[16,8]{1,0:T(8,128)S(1)}, f32[16,8]{1,0:T(8,128)}, u32[]{:S(2)}) copy-start(f32[16,8]{1,0:T(8,128)} %get-tuple-element.62) | copy-start | bytes 1540
  266.7 66.5 %copy-start.18 = (f32[16,8,8]{0,2,1:T(8,128)S(1)}, f32[16,8,8]{0,2,1:T(8,128)}, u32[]{:S(2)}) copy-start(f32[16,8,8]{0,2,1:T(8,128)} %param.12) | copy-start | bytes 12292
  266.7 102.0 %copy-start.15 = (f32[16,1792]{1,0:T(8,128)S(1)}, f32[16,1792]{1,0:T(8,128)}, u32[]{:S(2)}) copy-start(f32[16,1792]{1,0:T(8,128)} %param.10) | copy-start | bytes 344068
  328.4 17.3 %all-to-all-start.1 = ((f32[8,8,1792]{2,0,1:T(8,128)}), f32[8,8,1792]{2,0,1:T(8,128)S(1)}, u32[]{:S(2)}, u32[]{:S(2)}) async-start(f32[8,8,1792]{2,0,1:T(8,128)} %get-tuple-element.225), calls=%async_computation.2 | async-start | bytes 917504 | tf_op jit(solution)/shard_map/all_to_all | solution.py:148
  331.9 36.7 %reduce-scatter.7.cloned.1.call-start = ((), (), s32[]{:S(2)}) async-start(), calls=%async_computation.9 | async-start | bytes 573440 | tf_op jit(solution)/shard_map/reduce_scatter | solution.py:149
  346.6 69.9 %copy-start.28 = (f32[8]{0:T(128)}, f32[8]{0:T(128)S(1)}, u32[]{:S(2)}) copy-start(f32[8]{0:T(128)S(1)} %multiply_reduce_fusion.48) | copy-start | bytes 100
  348.1 68.4 %copy-start.49 = (f32[8,1]{0,1:T(1,128)}, f32[8,1]{0,1:T(1,128)S(1)}, u32[]{:S(2)}) copy-start(f32[8,1]{0,1:T(1,128)S(1)} %get-tuple-element.310) | copy-start | bytes 100
  348.1 68.4 %copy-start.50 = (f32[8,1]{0,1:T(1,128)}, f32[8,1]{0,1:T(1,128)S(1)}, u32[]{:S(2)}) copy-start(f32[8,1]{0,1:T(1,128)S(1)} %get-tuple-element.311) | copy-start | bytes 100
  348.1 68.4 %copy-start.51 = (f32[8,1]{0,1:T(1,128)}, f32[8,1]{0,1:T(1,128)S(1)}, u32[]{:S(2)}) copy-start(f32[8,1]{0,1:T(1,128)S(1)} %get-tuple-element.312) | copy-start | bytes 100
  348.1 68.4 %copy-start.52 = (f32[8,1]{0,1:T(1,128)}, f32[8,1]{0,1:T(1,128)S(1)}, u32[]{:S(2)}) copy-start(f32[8,1]{0,1:T(1,128)S(1)} %get-tuple-element.313) | copy-start | bytes 100
  348.1 132.4 %copy-start.29 = (f32[8]{0:T(128)}, f32[8]{0:T(128)S(1)}, u32[]{:S(2)}) copy-start(f32[8]{0:T(128)S(1)} %get-tuple-element.308) | copy-start | bytes 100
  348.1 132.4 %copy-start.30 = (f32[8]{0:T(128)}, f32[8]{0:T(128)S(1)}, u32[]{:S(2)}) copy-start(f32[8]{0:T(128)S(1)} %get-tuple-element.309) | copy-start | bytes 100
  348.2 132.4 %copy-start.31 = (f32[8]{0:T(128)}, f32[8]{0:T(128)S(1)}, u32[]{:S(2)}) copy-start(f32[8]{0:T(128)S(1)} %get-tuple-element.332) | copy-start | bytes 100
  348.2 132.4 %copy-start.32 = (f32[8]{0:T(128)}, f32[8]{0:T(128)S(1)}, u32[]{:S(2)}) copy-start(f32[8]{0:T(128)S(1)} %get-tuple-element.333) | copy-start | bytes 100
  348.2 132.4 %copy-start.33 = (f32[8]{0:T(128)}, f32[8]{0:T(128)S(1)}, u32[]{:S(2)}) copy-start(f32[8]{0:T(128)S(1)} %get-tuple-element.334) | copy-start | bytes 100
  348.2 132.4 %copy-start.34 = (f32[8]{0:T(128)}, f32[8]{0:T(128)S(1)}, u32[]{:S(2)}) copy-start(f32[8]{0:T(128)S(1)} %get-tuple-element.335) | copy-start | bytes 100
  348.2 132.4 %copy-start.35 = (f32[8]{0:T(128)}, f32[8]{0:T(128)S(1)}, u32[]{:S(2)}) copy-start(f32[8]{0:T(128)S(1)} %get-tuple-element.336) | copy-start | bytes 100
  348.2 132.4 %copy-start.36 = (f32[8]{0:T(128)}, f32[8]{0:T(128)S(1)}, u32[]{:S(2)}) copy-start(f32[8]{0:T(128)S(1)} %get-tuple-element.352) | copy-start | bytes 100
  348.2 132.4 %copy-start.37 = (f32[8]{0:T(128)}, f32[8]{0:T(128)S(1)}, u32[]{:S(2)}) copy-start(f32[8]{0:T(128)S(1)} %get-tuple-element.353) | copy-start | bytes 100
  348.2 132.4 %copy-start.38 = (f32[8]{0:T(128)}, f32[8]{0:T(128)S(1)}, u32[]{:S(2)}) copy-start(f32[8]{0:T(128)S(1)} %get-tuple-element.354) | copy-start | bytes 100
  462.3 18.2 %all-to-all-start.2 = ((f32[8,8,1792]{2,1,0:T(8,128)}), f32[8,8,1792]{2,1,0:T(8,128)S(1)}, u32[]{:S(2)}, u32[]{:S(2)}) async-start(f32[8,8,1792]{2,1,0:T(8,128)} %bitcast.156), calls=%async_computation.5 | async-start | bytes 917504 | tf_op jit(solution)/shard_map/all_to_all | solution.py:144
  466.4 126.4 %reduce-scatter.9.cloned.1.call-start = ((), (), s32[]{:S(2)}) async-start(), calls=%async_computation.10 | async-start | bytes 1032192 | tf_op jit(solution)/shard_map/reduce_scatter | solution.py:150
  511.7 40.1 %copy-start.25 = (f32[16,8]{0,1:T(8,128)S(1)}, f32[16,8]{0,1:T(8,128)}, u32[]{:S(2)}) copy-start(f32[16,8]{0,1:T(8,128)} %copy.372) | copy-start | bytes 1540
  511.7 81.1 %copy-start.16 = (f32[16,1792]{1,0:T(8,128)S(1)}, f32[16,1792]{1,0:T(8,128)}, u32[]{:S(2)}) copy-start(f32[16,1792]{1,0:T(8,128)} %reduce-scatter.5.cloned.1.call-done) | copy-start | bytes 344068
  511.7 81.1 %copy-start.17 = (f32[16,1792]{1,0:T(8,128)S(1)}, f32[16,1792]{1,0:T(8,128)}, u32[]{:S(2)}) copy-start(f32[16,1792]{1,0:T(8,128)} %reduce-scatter.7.cloned.1.call-done) | copy-start | bytes 344068
  547.5 17.3 %all-to-all-start.3 = ((f32[8,8,1792]{2,0,1:T(8,128)}), f32[8,8,1792]{2,0,1:T(8,128)S(1)}, u32[]{:S(2)}, u32[]{:S(2)}) async-start(f32[8,8,1792]{2,0,1:T(8,128)} %get-tuple-element.224), calls=%async_computation.6 | async-start | bytes 917504 | tf_op jit(solution)/shard_map/all_to_all | solution.py:148
  551.0 41.8 %reduce-scatter.11.cloned.1.call-start = ((), (), s32[]{:S(2)}) async-start(), calls=%async_computation.11 | async-start | bytes 573440 | tf_op jit(solution)/shard_map/reduce_scatter | solution.py:149
  (37 other events, 845.2 us)
Sparse Core Ops, SparseCore 0:
  220.9 32.4 reduce-scatter.4
  346.7 21.8 reduce-scatter.6
  470.4 32.6 reduce-scatter.8
  565.8 22.6 reduce-scatter.10
